TPU v7x, 32 devices: a whole 2x2x4 slice. The times are simulated.
32 devices in a mesh: rows: 4 (over y, x), mp: 8 (over z, core).
Axes of the slice: x: 2, y: 2, z: 4, core: 2. Of those that a mesh axis runs over, the one named last changes fastest.
Arguments:
- inputs: bfloat16 [8192, 2048], P(('rows', 'mp')), may hold values from -6 to 6
- cotangent: bfloat16 [8192, 2048], P(('rows', 'mp')), may hold values from -6 to 6
- corpus_ids: int32 [4], P('rows'), may hold values from 0 to 3
- corpus_weight: float32 [4], replicated, may hold values from 0.5 to 2
- attn_gain: bfloat16 [2048], P(('rows', 'mp')), may hold values from 0.099609375 to 1.8984375
- qkv_weight: bfloat16 [2048, 1920], P(('rows', 'mp')), may hold values from -0.125 to 0.125
- out_weight: bfloat16 [1280, 2048], P(('rows', 'mp')), may hold values from -2.5 to 2.5
- ffn_gain: bfloat16 [2048], P(('rows', 'mp')), may hold values from 0.099609375 to 1.8984375
- gate_weight: bfloat16 [2048, 6144], P(None, 'mp'), may hold values from -0.125 to 0.125
- up_weight: bfloat16 [2048, 6144], P(None, 'mp'), may hold values from -0.125 to 0.125
- down_weight: bfloat16 [6144, 2048], P('mp'), may hold values from -0.078125 to 0.078125
Outputs:
- outputs: bfloat16 [8192, 2048], P(('rows', 'mp'))
- input_grad: float32 [8192, 2048], P(('rows', 'mp'))
- qkv_grad: float32 [2048, 1920], P(('rows', 'mp'))
- proj_grad: float32 [1280, 2048], P(('rows', 'mp'))
- gate_grad: float32 [2048, 6144], P(None, 'mp')
- up_grad: float32 [2048, 6144], P(None, 'mp')
- down_grad: float32 [6144, 2048], P('mp')
- attn_gain_grad: float32 [2048], P(('rows', 'mp'))
- ffn_gain_grad: float32 [2048], P(('rows', 'mp'))
All inputs are finite; a program needn't handle non-finite values.
Results may differ from a plain program's by a relative error of at most 0.015.
Values may be sent and summed in bfloat16 or wider, within the bound.
A program may use at most 256 MiB of HBM per device.

v0:
```python
import jax
import jax.numpy as jnp
from jax import lax
from jax.sharding import PartitionSpec as P

HEADS = 20
KV_HEADS = 5
HEAD_DIM = 64
LEN = 2048
QBLOCK = 512
QBLOCKS = 4
EPS = 1e-05
THETA = 10000.0


def rotation(positions):
    half_dim = HEAD_DIM // 2
    freqs = jnp.exp(-jnp.log(THETA) * (2.0 * jnp.arange(half_dim, dtype=jnp.float32)) / HEAD_DIM)
    angles = positions.astype(jnp.float32)[:, None] * freqs[None, :]
    return (jnp.cos(angles), jnp.sin(angles))


def rotate(values_in, cosine, sine_part):
    half_dim = HEAD_DIM // 2
    first = values_in[..., :half_dim]
    second = values_in[..., half_dim:]
    return jnp.concatenate(
        [first * cosine - second * sine_part, second * cosine + first * sine_part], axis=-1
    )


def rotate_back(values_in, cosine, sine_part):
    half_dim = HEAD_DIM // 2
    first = values_in[..., :half_dim]
    second = values_in[..., half_dim:]
    return jnp.concatenate(
        [first * cosine + second * sine_part, second * cosine - first * sine_part], axis=-1
    )


def project_kv(normed, weight_kv, positions):
    row_count = normed.shape[0]
    kv_width = KV_HEADS * HEAD_DIM
    kv_raw = jnp.dot(normed, weight_kv, preferred_element_type=jnp.float32)
    cosine, sine_part = rotation(positions)
    keys_part = rotate(
        kv_raw[:, :kv_width].reshape(row_count, KV_HEADS, HEAD_DIM),
        cosine[:, None, :],
        sine_part[:, None, :],
    )
    return jnp.concatenate(
        [keys_part.reshape(row_count, kv_width), kv_raw[:, kv_width:]], axis=1
    ).astype(jnp.bfloat16)


def key_slices(kv_all, seq_start, kv_head, length):
    keys_part = lax.dynamic_slice(kv_all, (seq_start, kv_head * HEAD_DIM), (length, HEAD_DIM))
    values_part = lax.dynamic_slice(
        kv_all, (seq_start, (KV_HEADS + kv_head) * HEAD_DIM), (length, HEAD_DIM)
    )
    return (keys_part, values_part)


def masked_scores(queries, keys_part, block_index, length):
    scores = jnp.einsum(
        "qd,kd->qk", queries, keys_part, preferred_element_type=jnp.float32
    ) * HEAD_DIM ** (-0.5)
    allowed = jnp.arange(length)[None, :] <= block_index * QBLOCK + jnp.arange(QBLOCK)[:, None]
    return jnp.where(allowed, scores, -1e30)


def forward_branch(block_index):
    length = (block_index + 1) * QBLOCK

    def branch(queries, kv_all, seq_start, kv_head):
        keys_part, values_part = key_slices(kv_all, seq_start, kv_head, length)
        scores = masked_scores(queries, keys_part, block_index, length)
        row_max = jnp.max(scores, axis=1, keepdims=True)
        exponent = jnp.exp(scores - row_max)
        row_total = jnp.sum(exponent, axis=1, keepdims=True)
        probabilities = (exponent / row_total).astype(jnp.bfloat16)
        output = jnp.dot(probabilities, values_part, preferred_element_type=jnp.float32).astype(
            jnp.bfloat16
        )
        return (output, (row_max + jnp.log(row_total))[:, 0])

    return branch


def backward_branch(block_index):
    length = (block_index + 1) * QBLOCK

    def branch(queries, grad_output, log_total, kv_all, seq_start, kv_head):
        keys_part, values_part = key_slices(kv_all, seq_start, kv_head, length)
        scores = masked_scores(queries, keys_part, block_index, length)
        probabilities = jnp.exp(scores - log_total[:, None])
        grad_probs = jnp.einsum(
            "qd,kd->qk", grad_output, values_part, preferred_element_type=jnp.float32
        )
        row_delta = jnp.sum(probabilities * grad_probs, axis=1, keepdims=True)
        grad_scores = (probabilities * (grad_probs - row_delta)).astype(jnp.bfloat16)
        grad_queries = jnp.dot(
            grad_scores, keys_part, preferred_element_type=jnp.float32
        ) * HEAD_DIM ** (-0.5)
        grad_keys = jnp.einsum(
            "qk,qd->kd", grad_scores, queries, preferred_element_type=jnp.float32
        ) * HEAD_DIM ** (-0.5)
        grad_values = jnp.einsum(
            "qk,qd->kd",
            probabilities.astype(jnp.bfloat16),
            grad_output,
            preferred_element_type=jnp.float32,
        )
        padding = ((0, LEN - length), (0, 0))
        return (grad_queries, jnp.pad(grad_keys, padding), jnp.pad(grad_values, padding))

    return branch


def add_window(target, update, start_row, start_col):
    current = lax.dynamic_slice(target, (start_row, start_col), update.shape)
    return lax.dynamic_update_slice(target, current + update, (start_row, start_col))


def on_device(
    inputs,
    cotangent,
    corpus_ids,
    corpus_weight,
    attn_gain,
    qkv_weight,
    out_weight,
    ffn_gain,
    gate_weight,
    up_weight,
    down_weight,
):
    tok_dev = inputs.shape[0]
    group_rows = tok_dev * lax.axis_size("mp")
    offset = lax.axis_index("mp") * tok_dev
    seq_group = corpus_ids.shape[0]
    corpora_count = corpus_weight.shape[0]
    sequences_all = seq_group * lax.axis_size("rows")
    q_width = HEADS * HEAD_DIM
    kv_width = KV_HEADS * HEAD_DIM
    group_size = HEADS // KV_HEADS
    model_width = inputs.shape[1]
    tiles_dev = HEADS * QBLOCKS // lax.axis_size("mp")
    first_tile = lax.axis_index("mp") * tiles_dev
    chosen = (corpus_ids[:, None] == jnp.arange(corpora_count)[None, :]).astype(jnp.float32)
    counts = lax.psum(jnp.sum(chosen, axis=0), "rows")
    count_seq = jnp.sum(chosen * counts[None, :], axis=1)
    weight_seq = jnp.sum(chosen * corpus_weight[None, :], axis=1)
    seq_scale = weight_seq * sequences_all / (corpora_count * count_seq)
    qkv_full, out_full, gain_one, gain_two = (
        lax.all_gather(qkv_weight, ("rows", "mp"), axis=0, tiled=True),
        lax.all_gather(out_weight, ("rows", "mp"), axis=0, tiled=True),
        lax.all_gather(attn_gain, ("rows", "mp"), axis=0, tiled=True),
        lax.all_gather(ffn_gain, ("rows", "mp"), axis=0, tiled=True),
    )
    gain_one = gain_one.astype(jnp.float32)
    gain_two = gain_two.astype(jnp.float32)
    weight_kv = qkv_full[:, q_width:]
    residual = inputs.astype(jnp.float32)
    inverse_one = lax.rsqrt(jnp.mean(residual * residual, axis=-1, keepdims=True) + EPS)
    normed_one = (residual * inverse_one * gain_one).astype(jnp.bfloat16)
    local_pos = (offset + jnp.arange(tok_dev)) % LEN
    normed_all, kv_all = (
        lax.all_gather(normed_one, "mp", axis=0, tiled=True),
        lax.all_gather(project_kv(normed_one, weight_kv, local_pos), "mp", axis=0, tiled=True),
    )
    count_items = tiles_dev * seq_group
    forward_list = [forward_branch(b) for b in range(QBLOCKS)]
    backward_list = [backward_branch(b) for b in range(QBLOCKS)]

    def item_info(item_index):
        tile_index = first_tile + item_index // seq_group
        seq_start = item_index % seq_group * LEN
        head_index = tile_index // QBLOCKS
        block_index = tile_index % QBLOCKS
        return (head_index, block_index, seq_start, seq_start + block_index * QBLOCK)

    def forward_item(partial_value, item_index):
        head_index, block_index, seq_start, row_start = item_info(item_index)
        rows_in = lax.dynamic_slice(normed_all, (row_start, 0), (QBLOCK, model_width))
        weight_q = lax.dynamic_slice(qkv_full, (0, head_index * HEAD_DIM), (model_width, HEAD_DIM))
        raw_queries = jnp.dot(rows_in, weight_q, preferred_element_type=jnp.float32)
        cosine, sine_part = rotation(block_index * QBLOCK + jnp.arange(QBLOCK))
        queries = rotate(raw_queries, cosine, sine_part).astype(jnp.bfloat16)
        output, log_total = lax.switch(
            block_index, forward_list, queries, kv_all, seq_start, head_index // group_size
        )
        weight_o = lax.dynamic_slice(out_full, (head_index * HEAD_DIM, 0), (HEAD_DIM, model_width))
        partial_value = add_window(
            partial_value,
            jnp.dot(output, weight_o, preferred_element_type=jnp.float32),
            row_start,
            0,
        )
        return (partial_value, (queries, output, log_total))

    attn_partial, (kept_queries, kept_outputs, kept_totals) = lax.scan(
        forward_item, jnp.zeros((group_rows, model_width), jnp.float32), jnp.arange(count_items)
    )
    attn_sum = lax.psum_scatter(attn_partial, "mp", scatter_dimension=0, tiled=True)
    middle = residual + attn_sum
    inverse_two = lax.rsqrt(jnp.mean(middle * middle, axis=-1, keepdims=True) + EPS)
    normed_two = (middle * inverse_two * gain_two).astype(jnp.bfloat16)
    normed_mid = lax.all_gather(normed_two, "mp", axis=0, tiled=True)
    gate_val = jnp.dot(normed_mid, gate_weight, preferred_element_type=jnp.float32)
    up_val = jnp.dot(normed_mid, up_weight, preferred_element_type=jnp.float32)
    hidden = (jax.nn.silu(gate_val) * up_val).astype(jnp.bfloat16)
    ffn_part = jnp.dot(hidden, down_weight, preferred_element_type=jnp.float32)
    ffn_sum = lax.psum_scatter(
        ffn_part.astype(jnp.bfloat16), "mp", scatter_dimension=0, tiled=True
    ).astype(jnp.float32)
    outputs = (middle + ffn_sum).astype(jnp.bfloat16)
    seq_local = (offset + jnp.arange(tok_dev)) // LEN
    token_scale = jnp.sum(
        (seq_local[:, None] == jnp.arange(seq_group)[None, :]).astype(jnp.float32)
        * seq_scale[None, :],
        axis=1,
    )
    grad_out = cotangent.astype(jnp.float32) * token_scale[:, None]
    grad_all = lax.all_gather(grad_out.astype(jnp.bfloat16), "mp", axis=0, tiled=True)
    grad_hidden = jnp.einsum("td,fd->tf", grad_all, down_weight, preferred_element_type=jnp.float32)
    down_grad = jnp.einsum("tf,td->fd", hidden, grad_all, preferred_element_type=jnp.float32)
    sigmoid_val = jax.nn.sigmoid(gate_val)
    grad_gate = (
        grad_hidden * up_val * (sigmoid_val * (1.0 + gate_val * (1.0 - sigmoid_val)))
    ).astype(jnp.bfloat16)
    grad_up = (grad_hidden * (gate_val * sigmoid_val)).astype(jnp.bfloat16)
    gate_grad = jnp.einsum("td,tf->df", normed_mid, grad_gate, preferred_element_type=jnp.float32)
    up_grad = jnp.einsum("td,tf->df", normed_mid, grad_up, preferred_element_type=jnp.float32)
    mid_partial = jnp.einsum(
        "tf,df->td", grad_gate, gate_weight, preferred_element_type=jnp.float32
    )
    mid_partial = mid_partial + jnp.einsum(
        "tf,df->td", grad_up, up_weight, preferred_element_type=jnp.float32
    )
    grad_normed_two = lax.psum_scatter(mid_partial, "mp", scatter_dimension=0, tiled=True)
    scaled_two = grad_normed_two * gain_two
    ffn_gain_part = jnp.sum(grad_normed_two * middle * inverse_two, axis=0)
    grad_middle = (
        grad_out
        + inverse_two * scaled_two
        - middle * inverse_two**3 * jnp.mean(scaled_two * middle, axis=-1, keepdims=True)
    )
    grad_attn_all = lax.all_gather(grad_middle.astype(jnp.bfloat16), "mp", axis=0, tiled=True)

    def backward_item(carried, item_index):
        input_partial, kv_partial, q_grad_w, o_grad_w = carried
        head_index, block_index, seq_start, row_start = item_info(item_index)
        queries = kept_queries[item_index]
        output = kept_outputs[item_index]
        log_total = kept_totals[item_index]
        grad_rows = lax.dynamic_slice(grad_attn_all, (row_start, 0), (QBLOCK, model_width))
        weight_o = lax.dynamic_slice(out_full, (head_index * HEAD_DIM, 0), (HEAD_DIM, model_width))
        grad_output = jnp.einsum(
            "td,hd->th", grad_rows, weight_o, preferred_element_type=jnp.float32
        ).astype(jnp.bfloat16)
        o_grad_w = add_window(
            o_grad_w,
            jnp.einsum("th,td->hd", output, grad_rows, preferred_element_type=jnp.float32),
            head_index * HEAD_DIM,
            0,
        )
        kv_head = head_index // group_size
        grad_queries, grad_keys, grad_values = lax.switch(
            block_index, backward_list, queries, grad_output, log_total, kv_all, seq_start, kv_head
        )
        cosine, sine_part = rotation(block_index * QBLOCK + jnp.arange(QBLOCK))
        grad_raw = rotate_back(grad_queries, cosine, sine_part).astype(jnp.bfloat16)
        rows_in = lax.dynamic_slice(normed_all, (row_start, 0), (QBLOCK, model_width))
        weight_q = lax.dynamic_slice(qkv_full, (0, head_index * HEAD_DIM), (model_width, HEAD_DIM))
        input_partial = add_window(
            input_partial,
            jnp.einsum("th,dh->td", grad_raw, weight_q, preferred_element_type=jnp.float32),
            row_start,
            0,
        )
        q_grad_w = add_window(
            q_grad_w,
            jnp.einsum("td,th->dh", rows_in, grad_raw, preferred_element_type=jnp.float32),
            0,
            head_index * HEAD_DIM,
        )
        kv_partial = add_window(kv_partial, grad_keys, seq_start, kv_head * HEAD_DIM)
        kv_partial = add_window(kv_partial, grad_values, seq_start, (KV_HEADS + kv_head) * HEAD_DIM)
        return ((input_partial, kv_partial, q_grad_w, o_grad_w), None)

    start_state = (
        jnp.zeros((group_rows, model_width), jnp.float32),
        jnp.zeros((group_rows, 2 * kv_width), jnp.float32),
        jnp.zeros((model_width, q_width), jnp.float32),
        jnp.zeros((q_width, model_width), jnp.float32),
    )
    (input_partial, kv_partial, q_grad_w, o_grad_w), unused = lax.scan(
        backward_item, start_state, jnp.arange(count_items)
    )
    input_sum, kv_sum = (
        lax.psum_scatter(input_partial, "mp", scatter_dimension=0, tiled=True),
        lax.psum_scatter(kv_partial, "mp", scatter_dimension=0, tiled=True),
    )
    cos_local, sin_local = rotation(local_pos)
    grad_keys_local = rotate_back(
        kv_sum[:, :kv_width].reshape(tok_dev, KV_HEADS, HEAD_DIM),
        cos_local[:, None, :],
        sin_local[:, None, :],
    )
    grad_kv = jnp.concatenate(
        [grad_keys_local.reshape(tok_dev, kv_width), kv_sum[:, kv_width:]], axis=1
    ).astype(jnp.bfloat16)
    grad_normed_one = input_sum + jnp.einsum(
        "tk,dk->td", grad_kv, weight_kv, preferred_element_type=jnp.float32
    )
    kv_grad_w = jnp.einsum("td,tk->dk", normed_one, grad_kv, preferred_element_type=jnp.float32)
    qkv_grad_full = jnp.concatenate([q_grad_w, kv_grad_w], axis=1)
    scaled_one = grad_normed_one * gain_one
    attn_gain_part = jnp.sum(grad_normed_one * residual * inverse_one, axis=0)
    input_grad = (
        grad_middle
        + inverse_one * scaled_one
        - residual * inverse_one**3 * jnp.mean(scaled_one * residual, axis=-1, keepdims=True)
    )
    qkv_grad, proj_grad, attn_gain_grad, ffn_gain_grad = (
        lax.psum_scatter(qkv_grad_full, ("rows", "mp"), scatter_dimension=0, tiled=True),
        lax.psum_scatter(o_grad_w, ("rows", "mp"), scatter_dimension=0, tiled=True),
        lax.psum_scatter(attn_gain_part, ("rows", "mp"), scatter_dimension=0, tiled=True),
        lax.psum_scatter(ffn_gain_part, ("rows", "mp"), scatter_dimension=0, tiled=True),
    )
    gate_grad, up_grad, down_grad = (
        lax.psum(gate_grad.astype(jnp.bfloat16), "rows").astype(jnp.float32),
        lax.psum(up_grad.astype(jnp.bfloat16), "rows").astype(jnp.float32),
        lax.psum(down_grad.astype(jnp.bfloat16), "rows").astype(jnp.float32),
    )
    return (
        outputs,
        input_grad,
        qkv_grad,
        proj_grad,
        gate_grad,
        up_grad,
        down_grad,
        attn_gain_grad,
        ffn_gain_grad,
    )


def solution(mesh):
    in_specs = (
        P(("rows", "mp"), None),
        P(("rows", "mp"), None),
        P("rows"),
        P(),
        P(("rows", "mp")),
        P(("rows", "mp"), None),
        P(("rows", "mp"), None),
        P(("rows", "mp")),
        P(None, "mp"),
        P(None, "mp"),
        P("mp", None),
    )
    out_specs = (
        P(("rows", "mp"), None),
        P(("rows", "mp"), None),
        P(("rows", "mp"), None),
        P(("rows", "mp"), None),
        P(None, "mp"),
        P(None, "mp"),
        P("mp", None),
        P(("rows", "mp")),
        P(("rows", "mp")),
    )
    return jax.shard_map(
        on_device, mesh=mesh, in_specs=in_specs, out_specs=out_specs, check_vma=False
    )
```

profile of v0, /device:TPU:0, one launch (start us, length us, event | category | flops | bytes accessed | tf_op | source)
XLA Modules:
  0.0 2238.0 jit_solution(10643275704402246868)
XLA Ops:
  10.4 43.2 %all-reduce.11 = (bf16[2048]{0:T(1024)(128)(2,1)S(1)}, bf16[2048]{0:T(1024)(128)(2,1)S(1)}) all-reduce(bf16[2048]{0:T(1024)(128)(2,1)S(1)} %dynamic-update-slice, bf16[2048]{0:T(1024)(128)(2,1)S(1)} %dynamic-update-slice.1), channel_id=1, replica_groups=mesh['rows'=4,'mp'=8] {'rows','mp'}, use_global_device_ids=true, to_apply=%add.6 | all-reduce | flops 4096 | bytes 16384
  59.7 29.9 %all-gather.10.cloned.1.call-done = bf16[2048,1920]{1,0:T(8,128)(2,1)} async-done(((bf16[64,1920]{1,0:T(8,128)(2,1)}), bf16[2048,1920]{1,0:T(8,128)(2,1)}) %all-gather.10.cloned.1.call-update) | async-done | bytes 7864336 | tf_op jit(solution)/shard_map/all_gather | solution.py:156
  97.7 58.8 %all-gather.14.cloned.1.call-done = bf16[1280,2048]{1,0:T(8,128)(2,1)} async-done(((bf16[40,2048]{1,0:T(8,128)(2,1)}), bf16[1280,2048]{1,0:T(8,128)(2,1)}) %all-gather.14.cloned.1.call-update) | async-done | bytes 5242896 | tf_op jit(solution)/shard_map/all_gather | solution.py:157
  156.5 82.6 %all-gather.8.cloned.1.call-done = bf16[2048,2048]{1,0:T(8,128)(2,1)} async-done(((bf16[256,2048]{1,0:T(8,128)(2,1)}), bf16[2048,2048]{1,0:T(8,128)(2,1)}) %all-gather.8.cloned.1.call-update) | async-done | bytes 8388624 | tf_op jit(solution)/shard_map/all_gather | solution.py:169
  239.1 34.5 %all-gather.12.cloned.1.call-done = bf16[2048,640]{1,0:T(8,128)(2,1)} async-done(((bf16[256,640]{1,0:T(8,128)(2,1)}), bf16[2048,640]{1,0:T(8,128)(2,1)}) %all-gather.12.cloned.1.call-update) | async-done | bytes 2621456 | tf_op jit(solution)/shard_map/all_gather | solution.py:170
  281.5 150.9 %while.42 = (s32[]{:T(128)}, f32[2048,2048]{1,0:T(8,128)}, bf16[10,512,64]{1,2,0:T(8,128)(2,1)}, bf16[10,512,64]{1,2,0:T(8,128)(2,1)}, f32[10,512]{1,0:T(8,128)S...) while((s32[]{:T(128)}, f32[2048,2048]{1,0:T(8,128)}, ...), condition=%wide.region_14.15_spmd, body=%wide.region_1.14_spmd.sunk | while | flops 547767360 | bytes 25982072 | solution.py:202
  432.5 169.8 %reduce-scatter.8.cloned.1.call-done = f32[256,2048]{1,0:T(8,128)} async-done(((f32[2048,2048]{1,0:T(8,128)}), f32[256,2048]{1,0:T(8,128)}) %reduce-scatter.8.cloned.1.call-update) | async-done | bytes 2097168 | tf_op jit(solution)/shard_map/reduce_scatter | solution.py:205
  607.7 9.9 psum.28
  622.9 64.7 %all-gather.16.cloned.1.call-done = bf16[2048,2048]{1,0:T(8,128)(2,1)} async-done(((bf16[256,2048]{1,0:T(8,128)(2,1)}), bf16[2048,2048]{1,0:T(8,128)(2,1)}) %all-gather.16.cloned.1.call-update) | async-done | bytes 8388624 | tf_op jit(solution)/shard_map/all_gather | solution.py:209
  687.6 11.8 fusion.167
  699.4 8.5 fusion.166
  707.9 62.5 %all-gather.18.cloned.1.call-done = bf16[2048,2048]{1,0:T(8,128)(2,1)} async-done(((bf16[256,2048]{1,0:T(8,128)(2,1)}), bf16[2048,2048]{1,0:T(8,128)(2,1)}) %all-gather.18.cloned.1.call-update) | async-done | bytes 8388624 | tf_op jit(solution)/shard_map/all_gather | solution.py:225
  770.4 15.7 multiply_convert_fusion.2
  786.1 13.3 fusion.168
  799.4 14.1 convolution_add_fusion.2
  813.6 10.8 convolution_convert_fusion
  824.5 156.0 %reduce-scatter.12.cloned.1.call-done = f32[256,2048]{1,0:T(8,128)} async-done(((f32[2048,2048]{1,0:T(8,128)}), f32[256,2048]{1,0:T(8,128)}) %reduce-scatter.12.cloned.1.call-update) | async-done | bytes 2097168 | tf_op jit(solution)/shard_map/reduce_scatter | solution.py:241
  983.3 87.6 %reduce-scatter.10.cloned.1.call-done = bf16[256,2048]{1,0:T(8,128)(2,1)} async-done(((bf16[2048,2048]{1,0:T(8,128)(2,1)}), bf16[256,2048]{1,0:T(8,128)(2,1)}) %reduce-scatter.10.cloned.1.call-update) | async-done | bytes 1048592 | tf_op jit(solution)/shard_map/reduce_scatter | solution.py:214
  1077.9 78.2 %all-gather.20.cloned.1.call-done = bf16[2048,2048]{1,0:T(8,128)(2,1)} async-done(((bf16[256,2048]{1,0:T(8,128)(2,1)}), bf16[2048,2048]{1,0:T(8,128)(2,1)}) %all-gather.20.cloned.1.call-update) | async-done | bytes 8388624 | tf_op jit(solution)/shard_map/all_gather | solution.py:249
  1177.5 293.2 %while.43 = (s32[]{:T(128)}, f32[2048,2048]{1,0:T(8,128)}, f32[2048,640]{0,1:T(8,128)}, f32[2048,1280]{0,1:T(8,128)}, f32[1280,2048]{1,0:T(8,128)}, /*index=5*/s...) while((s32[]{:T(128)}, f32[2048,2048]{1,0:T(8,128)}, ...), condition=%wide.region_32.33_spmd, body=%wide.region_23.32_spmd.sunk | while | flops 1220625536 | bytes 55792484 | solution.py:298
  1239.8 9.2 conditional.18
  1270.0 10.5 conditional.18
  1357.9 9.2 conditional.18
  1388.1 10.5 conditional.18
  1470.7 12.2 convolution_convert_fusion.1
  1501.3 11.6 copy.61
  1512.9 21.2 reduce-scatter.16.cloned.1.call-done
  1546.4 180.2 %all-reduce.15.cloned.1.call-done = (bf16[2048,768]{1,0:T(8,128)(2,1)}, bf16[2048,768]{1,0:T(8,128)(2,1)}, bf16[768,2048]{1,0:T(8,128)(2,1)}) async-done(((bf16[2048,768]{1,0:T(8,128)(2,1)}, bf16[2048,768]{1,0:T(8,128)(2,1)}, bf16[768,2048]{1,0:T(8,128)(2,1)}), (bf16[2048,768]{1,0:T(8,128)(2,1)}, bf16[2048,768]{1,0:T(8,128)(2,1)}, bf16[768,2048]{1,0:T(8,128)(2,1)})) %all-reduce.15.cloned.1.call-update) | async-done | bytes 9437200 | tf_op jit(solution)/shard_map/psum | solution.py:333
  1739.3 158.0 %reduce-scatter.14.cloned.1.call-done = f32[256,2048]{1,0:T(8,128)} async-done(((f32[2048,2048]{1,0:T(8,128)}), f32[256,2048]{1,0:T(8,128)}) %reduce-scatter.14.cloned.1.call-update) | async-done | bytes 2097168 | tf_op jit(solution)/shard_map/reduce_scatter | solution.py:302
  1902.3 38.8 %all-reduce.10 = (f32[2048]{0:T(1024)S(1)}, f32[2048]{0:T(1024)S(1)}) all-reduce(f32[2048]{0:T(1024)S(1)} %get-tuple-element.1396, f32[2048]{0:T(1024)S(1)} %copy-done.14), channel_id=9, replica_groups=mesh['rows'=4,'mp'=8] {'rows','mp'}, use_global_device_ids=true, to_apply=%region_42.43.clone | all-reduce | flops 4096 | bytes 32768
  1947.0 109.4 %reduce-scatter.20.cloned.1.call-done = f32[40,2048]{1,0:T(8,128)} async-done(((f32[1280,2048]{1,0:T(8,128)}), f32[40,2048]{1,0:T(8,128)}) %reduce-scatter.20.cloned.1.call-update) | async-done | bytes 327696 | tf_op jit(solution)/shard_map/reduce_scatter | solution.py:328
  2056.3 174.8 %reduce-scatter.18.cloned.1.call-done = f32[64,1920]{1,0:T(8,128)} async-done(((f32[2048,1920]{1,0:T(8,128)}), f32[64,1920]{1,0:T(8,128)}) %reduce-scatter.18.cloned.1.call-update) | async-done | bytes 491536 | tf_op jit(solution)/shard_map/reduce_scatter | solution.py:327
  (498 shorter events, 621.9 us)
Async XLA Ops:
  7.2 763.2 %copy-start = (bf16[768,2048]{1,0:T(8,128)(2,1)S(1)}, bf16[768,2048]{1,0:T(8,128)(2,1)}, u32[]{:S(2)}) copy-start(bf16[768,2048]{1,0:T(8,128)(2,1)} %param.33) | copy-start | bytes 9437188
  7.2 82.5 %all-gather.10.cloned.1.call-start = ((), (), s32[]{:S(2)}) async-start(), calls=%async_computation.8 | async-start | bytes 8110080 | tf_op jit(solution)/shard_map/all_gather | solution.py:156
  7.9 148.6 %all-gather.14.cloned.1.call-start = ((), (), s32[]{:S(2)}) async-start(), calls=%async_computation.10 | async-start | bytes 5406720 | tf_op jit(solution)/shard_map/all_gather | solution.py:157
  8.7 230.4 %all-gather.8.cloned.1.call-start = ((), (), s32[]{:S(2)}) async-start(), calls=%async_computation.7 | async-start | bytes 9437184 | tf_op jit(solution)/shard_map/all_gather | solution.py:169
  58.8 214.7 %all-gather.12.cloned.1.call-start = ((), (), s32[]{:S(2)}) async-start(), calls=%async_computation.9 | async-start | bytes 2949120 | tf_op jit(solution)/shard_map/all_gather | solution.py:170
  97.4 504.8 %reduce-scatter.8.cloned.1.call-start = ((), (), s32[]{:S(2)}) async-start(), calls=%async_computation.11 | async-start | bytes 18874368 | tf_op jit(solution)/shard_map/reduce_scatter | solution.py:205
  432.4 255.2 %all-gather.16.cloned.1.call-start = ((), (), s32[]{:S(2)}) async-start(), calls=%async_computation.12 | async-start | bytes 9437184 | tf_op jit(solution)/shard_map/all_gather | solution.py:209
  604.5 13.1 copy-start.23
  607.0 163.4 %all-gather.18.cloned.1.call-start = ((), (), s32[]{:S(2)}) async-start(), calls=%async_computation.14 | async-start | bytes 9437184 | tf_op jit(solution)/shard_map/all_gather | solution.py:225
  622.7 357.9 %reduce-scatter.12.cloned.1.call-start = ((), (), s32[]{:S(2)}) async-start(), calls=%async_computation.15 | async-start | bytes 18874368 | tf_op jit(solution)/shard_map/reduce_scatter | solution.py:241
  770.4 15.7 copy-start.21
  786.1 13.3 copy-start.24
  786.1 13.3 copy-start.22
  813.6 257.2 %reduce-scatter.10.cloned.1.call-start = ((), (), s32[]{:S(2)}) async-start(), calls=%async_computation.13 | async-start | bytes 9437184 | tf_op jit(solution)/shard_map/reduce_scatter | solution.py:214
  824.4 156.1 %copy-start.4 = (f32[256,2048]{1,0:T(8,128)S(1)}, f32[256,2048]{1,0:T(8,128)}, u32[]{:S(2)}) copy-start(f32[256,2048]{1,0:T(8,128)} %copy-done.3) | copy-start | bytes 6291460
  824.5 246.3 %copy-start.7 = (bf16[256,2048]{1,0:T(8,128)(2,1)S(1)}, bf16[256,2048]{1,0:T(8,128)(2,1)}, u32[]{:S(2)}) copy-start(bf16[256,2048]{1,0:T(8,128)(2,1)} %param.24) | copy-start | bytes 3145732
  824.5 331.6 %all-gather.20.cloned.1.call-start = ((), (), s32[]{:S(2)}) async-start(), calls=%async_computation.16 | async-start | bytes 9437184 | tf_op jit(solution)/shard_map/all_gather | solution.py:249
  1075.5 458.6 %reduce-scatter.16.cloned.1.call-start = ((), (), s32[]{:S(2)}) async-start(), calls=%async_computation.18 | async-start | bytes 5898240 | tf_op jit(solution)/shard_map/reduce_scatter | solution.py:303
  1470.7 12.2 copy-start.25
  1470.7 255.9 %all-reduce.15.cloned.1.call-start = ((), (), s32[]{:S(2)}) async-start(), calls=%async_computation.21 | async-start | bytes 18874368 | tf_op jit(solution)/shard_map/psum | solution.py:333
  1499.9 397.3 %reduce-scatter.14.cloned.1.call-start = ((), (), s32[]{:S(2)}) async-start(), calls=%async_computation.17 | async-start | bytes 18874368 | tf_op jit(solution)/shard_map/reduce_scatter | solution.py:302
  1500.7 555.7 %reduce-scatter.20.cloned.1.call-start = ((), (), s32[]{:S(2)}) async-start(), calls=%async_computation.20 | async-start | bytes 10813440 | tf_op jit(solution)/shard_map/reduce_scatter | solution.py:328
  1501.2 729.9 %reduce-scatter.18.cloned.1.call-start = ((), (), s32[]{:S(2)}) async-start(), calls=%async_computation.19 | async-start | bytes 16220160 | tf_op jit(solution)/shard_map/reduce_scatter | solution.py:327
  1501.3 34.8 %copy-start.10 = (f32[256,32]{0,1:T(8,128)S(1)}, f32[256,32]{0,1:T(8,128)}, u32[]{:S(2)}) copy-start(f32[256,32]{0,1:T(8,128)} %get-tuple-element.1491) | copy-start | bytes 98308
  1501.3 34.8 %copy-start.11 = (f32[256,32]{0,1:T(8,128)S(1)}, f32[256,32]{0,1:T(8,128)}, u32[]{:S(2)}) copy-start(f32[256,32]{0,1:T(8,128)} %get-tuple-element.1492) | copy-start | bytes 98308
  1501.3 34.9 %copy-start.6 = (bf16[256,2048]{1,0:T(8,128)(2,1)S(1)}, bf16[256,2048]{1,0:T(8,128)(2,1)}, u32[]{:S(2)}) copy-start(bf16[256,2048]{1,0:T(8,128)(2,1)} %fusion.148) | copy-start | bytes 3145732
  1735.7 161.5 %copy-start.5 = (bf16[256,2048]{1,0:T(8,128)(2,1)S(1)}, bf16[256,2048]{1,0:T(8,128)(2,1)}, u32[]{:S(2)}) copy-start(bf16[256,2048]{1,0:T(8,128)(2,1)} %param.23) | copy-start | bytes 3145732
  1735.7 161.5 %copy-start.13 = (f32[2048]{0:T(1024)S(1)}, f32[2048]{0:T(1024)}, u32[]{:S(2)}) copy-start(f32[2048]{0:T(1024)} %copy-done.12) | copy-start | bytes 24580
  1735.7 161.5 %copy-start.16 = (f32[256]{0:T(256)S(1)}, f32[256]{0:T(256)}, u32[]{:S(2)}) copy-start(f32[256]{0:T(256)} %copy-done.15) | copy-start | bytes 3076
  1739.2 163.1 %copy-start.14 = (f32[2048]{0:T(1024)S(1)}, f32[2048]{0:T(1024)}, u32[]{:S(2)}) copy-start(f32[2048]{0:T(1024)} %get-tuple-element.1394) | copy-start | bytes 24580
  1739.3 203.1 %copy-start.17 = (f32[256]{0:T(256)S(1)}, f32[256]{0:T(256)}, u32[]{:S(2)}) copy-start(f32[256]{0:T(256)} %get-tuple-element.1493) | copy-start | bytes 3076
  1942.3 288.8 %copy-start.1 = (bf16[768,2048]{1,0:T(8,128)(2,1)S(1)}, bf16[768,2048]{1,0:T(8,128)(2,1)}, u32[]{:S(2)}) copy-start(bf16[768,2048]{1,0:T(8,128)(2,1)} %param.33) | copy-start | bytes 9437188
  (10 other events, 61.3 us)
Sparse Core Ops, SparseCore 0:
  11.0 78.5 all-gather.9
  92.5 63.9 all-gather.13
  158.1 80.9 all-gather.7
  241.1 32.3 all-gather.11
  432.5 169.6 reduce-scatter.7
  607.1 80.4 all-gather.15
  689.8 80.5 all-gather.17
  813.7 166.7 reduce-scatter.11
  982.8 87.9 reduce-scatter.9
  1075.6 80.4 all-gather.19
  1470.8 63.3 reduce-scatter.15
  1538.4 188.0 all-reduce.14
  1728.9 168.2 reduce-scatter.13
  1899.9 156.3 reduce-scatter.19
  2062.8 168.3 reduce-scatter.17
where the time goes:
time: 2250 us; the launch traced here: 2240 us
  waiting for transfers between devices  1470 us (65%)
  matrix products  430 us (19%)
  other arithmetic  110 us (5%)
  blocking collectives  91.9 us (4%)
  local copies, waits for them, and re-layouts  82.2 us (4%)
  loops' own time  36 us (2%)
    psum x1, waiting for transfers between devices, on_device(): lax.psum(gate_grad.astype(jnp.bfloat16), 'rows').astype(jnp.float32)  180 us
    reduce_scatter x1, waiting for transfers between devices, on_device(): lax.psum_scatter(qkv_grad_full, ('rows', 'mp'), scatter_dimension=0, tile...  175 us
    reduce_scatter x1, waiting for transfers between devices, on_device(): lax.psum_scatter(attn_partial, 'mp', scatter_dimension=0, tiled=True)  170 us
    reduce_scatter x1, waiting for transfers between devices, on_device(): lax.psum_scatter(input_partial, 'mp', scatter_dimension=0, tiled=True)  158 us
    reduce_scatter x1, waiting for transfers between devices, on_device(): lax.psum_scatter(mid_partial, 'mp', scatter_dimension=0, tiled=True)  156 us
    reduce_scatter x1, waiting for transfers between devices, on_device(): lax.psum_scatter(o_grad_w, ('rows', 'mp'), scatter_dimension=0, tiled=True)  109 us
    reduce_scatter x1, waiting for transfers between devices, on_device(): lax.psum_scatter(ffn_part.astype(jnp.bfloat16), 'mp', scatter_dimension=0...  87.6 us
    all_gather x1, waiting for transfers between devices, on_device(): lax.all_gather(normed_one, 'mp', axis=0, tiled=True)  82.6 us
  transfers between devices with their start and end apart: 15, of which 15 were waited for; matrix products, arithmetic and copies ran while one was open for 6% of the time, Pallas kernels for 0%

commit v1 on v0

--- a/solution.py
+++ b/solution.py
@@ -154,7 +154,15 @@
     seq_scale = weight_seq * sequences_all / (corpora_count * count_seq)
     qkv_full, out_full, gain_one, gain_two = (
         lax.all_gather(qkv_weight, ("rows", "mp"), axis=0, tiled=True),
-        lax.all_gather(out_weight, ("rows", "mp"), axis=0, tiled=True),
+        jnp.concatenate(
+            lax.all_to_all(
+                jnp.stack([out_weight for _ in range(lax.axis_size(("rows", "mp")))]),
+                ("rows", "mp"),
+                0,
+                0,
+            ),
+            0,
+        ),
         lax.all_gather(attn_gain, ("rows", "mp"), axis=0, tiled=True),
         lax.all_gather(ffn_gain, ("rows", "mp"), axis=0, tiled=True),
     )

time: 2250 us -> 2270 us (level)
    all_to_all x0 -> x1, waiting for transfers between devices: none -> 135 us  [on_device(): lax.all_to_all(jnp.stack([out_weight for _ in range(lax.axis_size(('rows'...]
    all_gather x1, waiting for transfers between devices: 82.6 us -> 0.01 us  [on_device(): lax.all_gather(normed_one, 'mp', axis=0, tiled=True)]
    all_gather x1 -> x0, waiting for transfers between devices: 58.8 us -> none  [on_device(): lax.all_gather(out_weight, ('rows', 'mp'), axis=0, tiled=True)]
    all_gather x1, waiting for transfers between devices: 29.9 us -> 58.4 us  [on_device(): lax.all_gather(qkv_weight, ('rows', 'mp'), axis=0, tiled=True)]
  transfers between devices with their start and end apart: 15 -> 15, of which waited for: 15 -> 14; matrix products, arithmetic and copies ran while one was open for 6% -> 6% of each run, Pallas kernels for 0% -> 0%
where the time goes in v1:
time: 2270 us; the launch traced here: 2260 us
  waiting for transfers between devices  1490 us (66%)
  matrix products  429 us (19%)
  other arithmetic  110 us (5%)
  blocking collectives  91.4 us (4%)
  local copies, waits for them, and re-layouts  85.3 us (4%)
  loops' own time  36.2 us (2%)
    psum x1, waiting for transfers between devices, on_device(): lax.psum(gate_grad.astype(jnp.bfloat16), 'rows').astype(jnp.float32)  180 us
    reduce_scatter x1, waiting for transfers between devices, on_device(): lax.psum_scatter(qkv_grad_full, ('rows', 'mp'), scatter_dimension=0, tile...  175 us
    reduce_scatter x1, waiting for transfers between devices, on_device(): lax.psum_scatter(attn_partial, 'mp', scatter_dimension=0, tiled=True)  170 us
    reduce_scatter x1, waiting for transfers between devices, on_device(): lax.psum_scatter(input_partial, 'mp', scatter_dimension=0, tiled=True)  158 us
    reduce_scatter x1, waiting for transfers between devices, on_device(): lax.psum_scatter(mid_partial, 'mp', scatter_dimension=0, tiled=True)  156 us
    all_to_all x1, waiting for transfers between devices, on_device(): lax.all_to_all(jnp.stack([out_weight for _ in range(lax.axis_size(('rows'...  135 us
    reduce_scatter x1, waiting for transfers between devices, on_device(): lax.psum_scatter(o_grad_w, ('rows', 'mp'), scatter_dimension=0, tiled=True)  109 us
    reduce_scatter x1, waiting for transfers between devices, on_device(): lax.psum_scatter(ffn_part.astype(jnp.bfloat16), 'mp', scatter_dimension=0...  87.5 us
  transfers between devices with their start and end apart: 15, of which 14 were waited for; matrix products, arithmetic and copies ran while one was open for 6% of the time, Pallas kernels for 0%

profile of v1, /device:TPU:0, one launch (start us, length us, event | category | flops | bytes accessed | tf_op | source)
XLA Modules:
  0.0 2263.0 jit_solution(7586262063640482584)
XLA Ops:
  9.9 42.5 %all-reduce.11 = (bf16[2048]{0:T(1024)(128)(2,1)S(1)}, bf16[2048]{0:T(1024)(128)(2,1)S(1)}) all-reduce(bf16[2048]{0:T(1024)(128)(2,1)S(1)} %dynamic-update-slice, bf16[2048]{0:T(1024)(128)(2,1)S(1)} %dynamic-update-slice.1), channel_id=1, replica_groups=mesh['rows'=4,'mp'=8] {'rows','mp'}, use_global_device_ids=true, to_apply=%add.6 | all-reduce | flops 4096 | bytes 16384
  66.1 58.4 %all-gather.9.cloned.1.call-done = bf16[2048,1920]{1,0:T(8,128)(2,1)} async-done(((bf16[64,1920]{1,0:T(8,128)(2,1)}), bf16[2048,1920]{1,0:T(8,128)(2,1)}) %all-gather.9.cloned.1.call-update) | async-done | bytes 7864336 | tf_op jit(solution)/shard_map/all_gather | solution.py:156
  132.6 134.5 %all-to-all-done = bf16[32,40,2048]{2,1,0:T(8,128)(2,1)} async-done(((bf16[32,40,2048]{2,1,0:T(8,128)(2,1)}), bf16[32,40,2048]{2,1,0:T(8,128)(2,1)}, u32[]{:S(2)}, u32[]{:S(2)}) %all-to-all-start) | async-done | bytes 5242912 | tf_op jit(solution)/shard_map/all_to_all | solution.py:158
  267.1 32.0 %all-gather.11.cloned.1.call-done = bf16[2048,640]{1,0:T(8,128)(2,1)} async-done(((bf16[256,640]{1,0:T(8,128)(2,1)}), bf16[2048,640]{1,0:T(8,128)(2,1)}) %all-gather.11.cloned.1.call-update) | async-done | bytes 2621456 | tf_op jit(solution)/shard_map/all_gather | solution.py:178
  307.0 150.9 %while.42 = (s32[]{:T(128)}, f32[2048,2048]{1,0:T(8,128)}, bf16[10,512,64]{1,2,0:T(8,128)(2,1)}, bf16[10,512,64]{1,2,0:T(8,128)(2,1)}, f32[10,512]{1,0:T(8,128)S...) while((s32[]{:T(128)}, f32[2048,2048]{1,0:T(8,128)}, ...), condition=%wide.region_14.15_spmd, body=%wide.region_1.14_spmd.sunk | while | flops 547767360 | bytes 25982072 | solution.py:210
  458.0 169.8 %reduce-scatter.8.cloned.1.call-done = f32[256,2048]{1,0:T(8,128)} async-done(((f32[2048,2048]{1,0:T(8,128)}), f32[256,2048]{1,0:T(8,128)}) %reduce-scatter.8.cloned.1.call-update) | async-done | bytes 2097168 | tf_op jit(solution)/shard_map/reduce_scatter | solution.py:213
  633.3 9.9 psum.28
  648.8 64.4 %all-gather.13.cloned.1.call-done = bf16[2048,2048]{1,0:T(8,128)(2,1)} async-done(((bf16[256,2048]{1,0:T(8,128)(2,1)}), bf16[2048,2048]{1,0:T(8,128)(2,1)}) %all-gather.13.cloned.1.call-update) | async-done | bytes 8388624 | tf_op jit(solution)/shard_map/all_gather | solution.py:217
  713.2 11.8 fusion.167
  725.0 8.5 fusion.166
  733.5 62.3 %all-gather.15.cloned.1.call-done = bf16[2048,2048]{1,0:T(8,128)(2,1)} async-done(((bf16[256,2048]{1,0:T(8,128)(2,1)}), bf16[2048,2048]{1,0:T(8,128)(2,1)}) %all-gather.15.cloned.1.call-update) | async-done | bytes 8388624 | tf_op jit(solution)/shard_map/all_gather | solution.py:233
  795.8 15.7 multiply_convert_fusion.2
  811.5 13.3 fusion.168
  824.9 13.8 convolution_add_fusion.2
  838.8 10.8 convolution_convert_fusion
  849.7 156.0 %reduce-scatter.12.cloned.1.call-done = f32[256,2048]{1,0:T(8,128)} async-done(((f32[2048,2048]{1,0:T(8,128)}), f32[256,2048]{1,0:T(8,128)}) %reduce-scatter.12.cloned.1.call-update) | async-done | bytes 2097168 | tf_op jit(solution)/shard_map/reduce_scatter | solution.py:249
  1008.4 87.5 %reduce-scatter.10.cloned.1.call-done = bf16[256,2048]{1,0:T(8,128)(2,1)} async-done(((bf16[2048,2048]{1,0:T(8,128)(2,1)}), bf16[256,2048]{1,0:T(8,128)(2,1)}) %reduce-scatter.10.cloned.1.call-update) | async-done | bytes 1048592 | tf_op jit(solution)/shard_map/reduce_scatter | solution.py:222
  1103.0 78.2 %all-gather.17.cloned.1.call-done = bf16[2048,2048]{1,0:T(8,128)(2,1)} async-done(((bf16[256,2048]{1,0:T(8,128)(2,1)}), bf16[2048,2048]{1,0:T(8,128)(2,1)}) %all-gather.17.cloned.1.call-update) | async-done | bytes 8388624 | tf_op jit(solution)/shard_map/all_gather | solution.py:257
  1202.6 293.4 %while.43 = (s32[]{:T(128)}, f32[2048,2048]{1,0:T(8,128)}, f32[2048,640]{0,1:T(8,128)}, f32[2048,1280]{0,1:T(8,128)}, f32[1280,2048]{1,0:T(8,128)}, /*index=5*/s...) while((s32[]{:T(128)}, f32[2048,2048]{1,0:T(8,128)}, ...), condition=%wide.region_32.33_spmd, body=%wide.region_23.32_spmd.sunk | while | flops 1220625536 | bytes 55792484 | solution.py:306
  1264.9 9.2 conditional.18
  1295.1 10.5 conditional.18
  1383.0 9.2 conditional.18
  1413.2 10.5 conditional.18
  1496.1 12.2 convolution_convert_fusion.1
  1516.7 8.5 convolution_convert_fusion.3
  1526.6 11.6 copy.61
  1538.2 21.3 reduce-scatter.16.cloned.1.call-done
  1571.8 180.3 %all-reduce.15.cloned.1.call-done = (bf16[2048,768]{1,0:T(8,128)(2,1)}, bf16[2048,768]{1,0:T(8,128)(2,1)}, bf16[768,2048]{1,0:T(8,128)(2,1)}) async-done(((bf16[2048,768]{1,0:T(8,128)(2,1)}, bf16[2048,768]{1,0:T(8,128)(2,1)}, bf16[768,2048]{1,0:T(8,128)(2,1)}), (bf16[2048,768]{1,0:T(8,128)(2,1)}, bf16[2048,768]{1,0:T(8,128)(2,1)}, bf16[768,2048]{1,0:T(8,128)(2,1)})) %all-reduce.15.cloned.1.call-update) | async-done | bytes 9437200 | tf_op jit(solution)/shard_map/psum | solution.py:341
  1764.7 157.8 %reduce-scatter.14.cloned.1.call-done = f32[256,2048]{1,0:T(8,128)} async-done(((f32[2048,2048]{1,0:T(8,128)}), f32[256,2048]{1,0:T(8,128)}) %reduce-scatter.14.cloned.1.call-update) | async-done | bytes 2097168 | tf_op jit(solution)/shard_map/reduce_scatter | solution.py:310
  1927.7 39.0 %all-reduce.10 = (f32[2048]{0:T(1024)S(1)}, f32[2048]{0:T(1024)S(1)}) all-reduce(f32[2048]{0:T(1024)S(1)} %get-tuple-element.1396, f32[2048]{0:T(1024)S(1)} %copy-done.15), channel_id=9, replica_groups=mesh['rows'=4,'mp'=8] {'rows','mp'}, use_global_device_ids=true, to_apply=%region_42.43.clone | all-reduce | flops 4096 | bytes 32768
  1972.5 109.3 %reduce-scatter.20.cloned.1.call-done = f32[40,2048]{1,0:T(8,128)} async-done(((f32[1280,2048]{1,0:T(8,128)}), f32[40,2048]{1,0:T(8,128)}) %reduce-scatter.20.cloned.1.call-update) | async-done | bytes 327696 | tf_op jit(solution)/shard_map/reduce_scatter | solution.py:336
  2081.8 174.5 %reduce-scatter.18.cloned.1.call-done = f32[64,1920]{1,0:T(8,128)} async-done(((f32[2048,1920]{1,0:T(8,128)}), f32[64,1920]{1,0:T(8,128)}) %reduce-scatter.18.cloned.1.call-update) | async-done | bytes 491536 | tf_op jit(solution)/shard_map/reduce_scatter | solution.py:335
  (500 shorter events, 620.8 us)
Async XLA Ops:
  7.2 788.6 %copy-start = (bf16[768,2048]{1,0:T(8,128)(2,1)S(1)}, bf16[768,2048]{1,0:T(8,128)(2,1)}, u32[]{:S(2)}) copy-start(bf16[768,2048]{1,0:T(8,128)(2,1)} %param.33) | copy-start | bytes 9437188
  7.2 50.4 %copy-start.12 = (bf16[40,2048]{1,0:T(8,128)(2,1)S(1)}, bf16[40,2048]{1,0:T(8,128)(2,1)}, u32[]{:S(2)}) copy-start(bf16[40,2048]{1,0:T(8,128)(2,1)} %param.29) | copy-start | bytes 491524
  7.2 117.3 %all-gather.9.cloned.1.call-start = ((), (), s32[]{:S(2)}) async-start(), calls=%async_computation.9 | async-start | bytes 8110080 | tf_op jit(solution)/shard_map/all_gather | solution.py:156
  7.9 259.2 %all-gather.7.cloned.1.call-start = ((), (), s32[]{:S(2)}) async-start(), calls=%async_computation.8 | async-start | bytes 9437184 | tf_op jit(solution)/shard_map/all_gather | solution.py:177
  60.6 206.5 %all-to-all-start = ((bf16[32,40,2048]{2,1,0:T(8,128)(2,1)}), bf16[32,40,2048]{2,1,0:T(8,128)(2,1)}, u32[]{:S(2)}, u32[]{:S(2)}) async-start(bf16[32,40,2048]{2,1,0:T(8,128)(2,1)} %stack.2), calls=%async_computation | async-start | bytes 10485760 | tf_op jit(solution)/shard_map/all_to_all | solution.py:158
  65.2 234.0 %all-gather.11.cloned.1.call-start = ((), (), s32[]{:S(2)}) async-start(), calls=%async_computation.10 | async-start | bytes 2949120 | tf_op jit(solution)/shard_map/all_gather | solution.py:178
  132.2 495.6 %reduce-scatter.8.cloned.1.call-start = ((), (), s32[]{:S(2)}) async-start(), calls=%async_computation.11 | async-start | bytes 18874368 | tf_op jit(solution)/shard_map/reduce_scatter | solution.py:213
  458.0 255.2 %all-gather.13.cloned.1.call-start = ((), (), s32[]{:S(2)}) async-start(), calls=%async_computation.12 | async-start | bytes 9437184 | tf_op jit(solution)/shard_map/all_gather | solution.py:217
  630.0 13.1 copy-start.24
  632.6 163.2 %all-gather.15.cloned.1.call-start = ((), (), s32[]{:S(2)}) async-start(), calls=%async_computation.14 | async-start | bytes 9437184 | tf_op jit(solution)/shard_map/all_gather | solution.py:233
  648.2 357.4 %reduce-scatter.12.cloned.1.call-start = ((), (), s32[]{:S(2)}) async-start(), calls=%async_computation.15 | async-start | bytes 18874368 | tf_op jit(solution)/shard_map/reduce_scatter | solution.py:249
  795.8 15.7 copy-start.22
  811.5 13.3 copy-start.25
  811.5 13.3 copy-start.23
  838.7 257.2 %reduce-scatter.10.cloned.1.call-start = ((), (), s32[]{:S(2)}) async-start(), calls=%async_computation.13 | async-start | bytes 9437184 | tf_op jit(solution)/shard_map/reduce_scatter | solution.py:222
  849.6 156.1 %copy-start.4 = (f32[256,2048]{1,0:T(8,128)S(1)}, f32[256,2048]{1,0:T(8,128)}, u32[]{:S(2)}) copy-start(f32[256,2048]{1,0:T(8,128)} %copy-done.3) | copy-start | bytes 6291460
  849.6 246.3 %copy-start.7 = (bf16[256,2048]{1,0:T(8,128)(2,1)S(1)}, bf16[256,2048]{1,0:T(8,128)(2,1)}, u32[]{:S(2)}) copy-start(bf16[256,2048]{1,0:T(8,128)(2,1)} %param.24) | copy-start | bytes 3145732
  849.6 331.6 %all-gather.17.cloned.1.call-start = ((), (), s32[]{:S(2)}) async-start(), calls=%async_computation.16 | async-start | bytes 9437184 | tf_op jit(solution)/shard_map/all_gather | solution.py:257
  1100.6 458.9 %reduce-scatter.16.cloned.1.call-start = ((), (), s32[]{:S(2)}) async-start(), calls=%async_computation.18 | async-start | bytes 5898240 | tf_op jit(solution)/shard_map/reduce_scatter | solution.py:311
  1496.0 256.0 %all-reduce.15.cloned.1.call-start = ((), (), s32[]{:S(2)}) async-start(), calls=%async_computation.21 | async-start | bytes 18874368 | tf_op jit(solution)/shard_map/psum | solution.py:341
  1525.2 397.3 %reduce-scatter.14.cloned.1.call-start = ((), (), s32[]{:S(2)}) async-start(), calls=%async_computation.17 | async-start | bytes 18874368 | tf_op jit(solution)/shard_map/reduce_scatter | solution.py:310
  1525.8 555.9 %reduce-scatter.20.cloned.1.call-start = ((), (), s32[]{:S(2)}) async-start(), calls=%async_computation.20 | async-start | bytes 10813440 | tf_op jit(solution)/shard_map/reduce_scatter | solution.py:336
  1526.6 729.7 %reduce-scatter.18.cloned.1.call-start = ((), (), s32[]{:S(2)}) async-start(), calls=%async_computation.19 | async-start | bytes 16220160 | tf_op jit(solution)/shard_map/reduce_scatter | solution.py:335
  1526.6 34.9 %copy-start.10 = (f32[256,32]{0,1:T(8,128)S(1)}, f32[256,32]{0,1:T(8,128)}, u32[]{:S(2)}) copy-start(f32[256,32]{0,1:T(8,128)} %get-tuple-element.1491) | copy-start | bytes 98308
  1526.6 34.9 %copy-start.11 = (f32[256,32]{0,1:T(8,128)S(1)}, f32[256,32]{0,1:T(8,128)}, u32[]{:S(2)}) copy-start(f32[256,32]{0,1:T(8,128)} %get-tuple-element.1492) | copy-start | bytes 98308
  1526.6 34.9 %copy-start.6 = (bf16[256,2048]{1,0:T(8,128)(2,1)S(1)}, bf16[256,2048]{1,0:T(8,128)(2,1)}, u32[]{:S(2)}) copy-start(bf16[256,2048]{1,0:T(8,128)(2,1)} %fusion.148) | copy-start | bytes 3145732
  1761.1 161.4 %copy-start.5 = (bf16[256,2048]{1,0:T(8,128)(2,1)S(1)}, bf16[256,2048]{1,0:T(8,128)(2,1)}, u32[]{:S(2)}) copy-start(bf16[256,2048]{1,0:T(8,128)(2,1)} %param.23) | copy-start | bytes 3145732
  1761.1 161.4 %copy-start.14 = (f32[2048]{0:T(1024)S(1)}, f32[2048]{0:T(1024)}, u32[]{:S(2)}) copy-start(f32[2048]{0:T(1024)} %copy-done.13) | copy-start | bytes 24580
  1761.2 161.4 %copy-start.17 = (f32[256]{0:T(256)S(1)}, f32[256]{0:T(256)}, u32[]{:S(2)}) copy-start(f32[256]{0:T(256)} %copy-done.16) | copy-start | bytes 3076
  1764.7 162.9 %copy-start.15 = (f32[2048]{0:T(1024)S(1)}, f32[2048]{0:T(1024)}, u32[]{:S(2)}) copy-start(f32[2048]{0:T(1024)} %get-tuple-element.1394) | copy-start | bytes 24580
  1764.7 203.1 %copy-start.18 = (f32[256]{0:T(256)S(1)}, f32[256]{0:T(256)}, u32[]{:S(2)}) copy-start(f32[256]{0:T(256)} %get-tuple-element.1493) | copy-start | bytes 3076
  1967.8 288.5 %copy-start.1 = (bf16[768,2048]{1,0:T(8,128)(2,1)S(1)}, bf16[768,2048]{1,0:T(8,128)(2,1)}, u32[]{:S(2)}) copy-start(bf16[768,2048]{1,0:T(8,128)(2,1)} %param.33) | copy-start | bytes 9437188
  (11 other events, 73.5 us)
Sparse Core Ops, SparseCore 0:
  11.1 113.3 all-gather.8
  126.1 138.7 all-gather.6
  267.1 32.0 all-gather.10
  458.1 169.6 reduce-scatter.7
  632.7 80.4 all-gather.12
  715.2 80.5 all-gather.14
  838.8 166.7 reduce-scatter.11
  1007.9 87.9 reduce-scatter.9
  1100.7 80.4 all-gather.16
  1496.1 63.3 reduce-scatter.15
  1563.9 188.0 all-reduce.14
  1754.3 168.2 reduce-scatter.13
  1925.4 156.2 reduce-scatter.19
  2088.2 168.0 reduce-scatter.17
